TPU v7x, 32 devices: a whole 2x2x4 slice. The times are simulated.
32 devices in a mesh: band: 4 (over x, core), grid: 8 (over z, y).
Axes of the slice: x: 2, y: 2, z: 4, core: 2. Of those that a mesh axis runs over, the one named last changes fastest.
Arguments:
- states: float32 [64, 64, 8, 128], P('band', 'grid'), may hold values from -6 to 6
- potential: float32 [64, 8, 128], P('grid'), may hold values from -1 to 1
- proj_index: int32 [16, 128], replicated, may hold values from 0 to 65535, as said below
- proj_value: float32 [16, 128], replicated, may hold values from 0 to 1
- proj_strength: float32 [16], replicated, may hold values from 0.5 to 4
Outputs:
- filtered: float32 [64, 64, 8, 128], P('band', 'grid')
- gram: float32 [64, 64], P('band')
- hamiltonian: float32 [64, 64], P('band')
Inputs may be any that keep to these rules, and one draw needn't show every extreme that they name: `proj_index`: along the first grid dimension every support point lies within 8 planes of its atom's centre plane.
All inputs are finite; a program needn't handle non-finite values.
Results may differ from a plain program's by a relative error of at most 0.0001.
Values sent between devices are 32-bit elements; how exact they have to be, the bound alone decides.
A program may use at most 64 MiB of HBM per device.

v0:
```python
import jax
import jax.numpy as jnp
from jax import lax
from jax.sharding import PartitionSpec as P

RADIUS = 4
DEGREE = 4
stencil_weights = (-205.0 / 72.0, 1.6, -0.2, 8.0 / 315.0, -1.0 / 560.0)
filter_centre = 10.0
filter_half = 6.0


def padded_2(block, sides, width):
    for axis, dim in sides:
        count = lax.axis_size(axis)
        forward = [(i, i + 1) for i in range(count - 1)]
        backward = [(target, source) for source, target in forward]
        low = lax.ppermute(
            lax.slice_in_dim(block, block.shape[dim] - width, None, axis=dim), axis, forward
        )
        high = lax.ppermute(lax.slice_in_dim(block, 0, width, axis=dim), axis, backward)
        block = jnp.concatenate([low, block, high], axis=dim)
    return block


def kinetic(padded):
    extent = padded.shape[-3] - 2 * RADIUS
    middle = padded[..., RADIUS : RADIUS + extent, :, :]
    grid_rows = middle.shape[-2]
    grid_cols = middle.shape[-1]
    pad_widths = [(0, 0)] * (middle.ndim - 2) + [(RADIUS, RADIUS), (RADIUS, RADIUS)]
    padded_yz = jnp.pad(middle, pad_widths)
    summed = 3.0 * stencil_weights[0] * middle
    for shift_by in range(1, RADIUS + 1):
        neighbours = (
            padded[..., RADIUS + shift_by : RADIUS + shift_by + extent, :, :]
            + padded[..., RADIUS - shift_by : RADIUS - shift_by + extent, :, :]
        )
        neighbours = (
            neighbours
            + padded_yz[
                ..., RADIUS + shift_by : RADIUS + shift_by + grid_rows, RADIUS : RADIUS + grid_cols
            ]
            + padded_yz[
                ..., RADIUS - shift_by : RADIUS - shift_by + grid_rows, RADIUS : RADIUS + grid_cols
            ]
        )
        neighbours = (
            neighbours
            + padded_yz[
                ..., RADIUS : RADIUS + grid_rows, RADIUS + shift_by : RADIUS + shift_by + grid_cols
            ]
            + padded_yz[
                ..., RADIUS : RADIUS + grid_rows, RADIUS - shift_by : RADIUS - shift_by + grid_cols
            ]
        )
        summed = summed + stencil_weights[shift_by] * neighbours
    return -0.5 * summed


def inner_rows(left, right):
    return lax.dot_general(
        left,
        right,
        (((1,), (1,)), ((), ())),
        precision=lax.Precision.HIGHEST,
        preferred_element_type=jnp.float32,
    )


def per_device(states, potential, proj_index, proj_value, proj_strength):
    state_count, planes, grid_rows, grid_cols = states.shape
    points = planes * grid_rows * grid_cols
    atom_count = proj_index.shape[0]
    offset = lax.axis_index("grid") * points
    local_idx = proj_index - offset
    inside = (local_idx >= 0) & (local_idx < points)
    safe_idx = jnp.where(inside, local_idx, 0)
    weights = jnp.where(inside, proj_value, 0.0)
    atom_rows = jnp.broadcast_to(jnp.arange(atom_count, dtype=jnp.int32)[:, None], safe_idx.shape)
    projector = jnp.zeros((atom_count, points), jnp.float32).at[atom_rows, safe_idx].add(weights)

    def apply_h(field):
        padded = padded_2(field, (("grid", 1),), RADIUS)
        kinetic_v = kinetic(padded)
        flat_v = field.reshape(state_count, points)
        partial_value = inner_rows(flat_v, projector)
        coeffs = lax.psum(partial_value, "grid")
        scaled = coeffs * proj_strength[None, :]
        nonlocal_v = jnp.dot(
            scaled, projector, precision=lax.Precision.HIGHEST, preferred_element_type=jnp.float32
        )
        return kinetic_v + potential * field + nonlocal_v.reshape(field.shape)

    previous = states
    current = (apply_h(states) - filter_centre * states) / filter_half
    for degree_k in range(1, DEGREE):
        following = 2.0 * (apply_h(current) - filter_centre * current) / filter_half - previous
        previous = current
        current = following
    images = apply_h(current)
    flat_y = current.reshape(state_count, points)
    flat_h = images.reshape(state_count, points)
    total_points = float(points * lax.axis_size("grid"))
    gathered = lax.all_gather(flat_y, "band", axis=0, tiled=True)
    partial_blocks = jnp.stack([inner_rows(flat_y, gathered), inner_rows(flat_h, gathered)])
    blocks = lax.psum(partial_blocks, "grid")
    gram = blocks[0] / total_points
    hamiltonian = blocks[1] / total_points
    return (current, gram, hamiltonian)


def solution(mesh):
    in_specs = (P("band", "grid", None, None), P("grid", None, None), P(), P(), P())
    out_specs = (P("band", "grid", None, None), P("band", None), P("band", None))
    return jax.shard_map(
        per_device, mesh=mesh, in_specs=in_specs, out_specs=out_specs, check_vma=False
    )
```

profile of v0, /device:TPU:0, one launch (start us, length us, event | category | flops | bytes accessed | tf_op | source)
XLA Modules:
  0.0 211.4 jit_solution(2648983875373184538)
XLA Ops:
  8.4 4.9 %collective-permute-start.1 = (f32[16,4,8,128]{3,2,1,0:T(8,128)S(1)}, f32[16,4,8,128]{3,2,1,0:T(8,128)S(1)}, u32[]{:S(2)}, u32[]{:S(2)}) collective-permute-start(f32[16,4,8,128]{3,2,1,0:T(8,128)S(1)} %get-tuple-element.14), channel_id=1, source_target_pairs={{0,1},{1,2},{2,3},{3,4},{4,5},{5,6},{6,7},{8,9},{9,10},{10,11},{11... | collective-permute-start | bytes 786440 | tf_op jit(solution)/shard_map/ppermute | solution.py:18
  13.3 1.3 collective-permute-start
  17.5 14.1 %scatter_custom_fusion = f32[131072]{0:T(1024)S(1)} fusion(s32[2048]{0:T(1024)S(1)} %select_bitcast_fusion, f32[2048]{0:T(1024)S(1)} %select_bitcast_fusion.1, f32[]{:T(128)} %constant.17.clone.1), kind=kCustom, calls=%fused_computation.348 | custom fusion | flops 2048 | bytes 524292
  32.7 23.2 %psum.42 = f32[16,16]{0,1:T(8,128)S(1)} all-reduce(f32[16,16]{0,1:T(8,128)S(1)} %convolution_bitcast_fusion.5), channel_id=1, replica_groups=mesh['band'=4,'grid'=8] {'grid'}, use_global_device_ids=true, to_apply=%region_1.2 | all-reduce | flops 256 | bytes 2048 | tf_op jit(solution)/shard_map/psum | solution.py:88
  56.9 1.2 broadcast_multiply_fusion
  58.8 1.3 collective-permute-start.3
  60.1 1.3 collective-permute-start.2
  62.4 20.4 %psum.43 = f32[16,16]{0,1:T(8,128)S(1)} all-reduce(f32[16,16]{0,1:T(8,128)S(1)} %fusion.189), channel_id=1, replica_groups=mesh['band'=4,'grid'=8] {'grid'}, use_global_device_ids=true, to_apply=%region_2.3 | all-reduce | flops 256 | bytes 2048 | tf_op jit(solution)/shard_map/psum | solution.py:88
  83.6 1.3 fusion.113
  85.0 1.3 collective-permute-start.5
  86.3 1.3 collective-permute-start.4
  88.6 20.4 %psum.44 = f32[16,16]{0,1:T(8,128)S(1)} all-reduce(f32[16,16]{0,1:T(8,128)S(1)} %fusion.186), channel_id=1, replica_groups=mesh['band'=4,'grid'=8] {'grid'}, use_global_device_ids=true, to_apply=%region_3.4 | all-reduce | flops 256 | bytes 2048 | tf_op jit(solution)/shard_map/psum | solution.py:88
  109.8 1.3 fusion.79
  111.1 1.7 collective-permute-start.7
  112.8 1.3 collective-permute-start.6
  115.1 20.2 %psum.45 = f32[16,16]{0,1:T(8,128)S(1)} all-reduce(f32[16,16]{0,1:T(8,128)S(1)} %fusion.183), channel_id=1, replica_groups=mesh['band'=4,'grid'=8] {'grid'}, use_global_device_ids=true, to_apply=%region_4.5 | all-reduce | flops 256 | bytes 2048 | tf_op jit(solution)/shard_map/psum | solution.py:88
  136.2 1.3 fusion.45
  138.7 1.5 collective-permute-start.9
  140.2 1.3 collective-permute-start.8
  142.4 21.0 %psum.46 = f32[16,16]{0,1:T(8,128)S(1)} all-reduce(f32[16,16]{0,1:T(8,128)S(1)} %fusion.213), channel_id=1, replica_groups=mesh['band'=4,'grid'=8] {'grid'}, use_global_device_ids=true, to_apply=%region_5.6 | all-reduce | flops 256 | bytes 2048 | tf_op jit(solution)/shard_map/psum | solution.py:88
  164.3 1.3 fusion.11
  165.6 3.5 %convolution_bitcast_fusion.7 = f32[1,16,64]{2,1,0:T(8,128)S(1)} fusion(f32[64,8192]{1,0:T(8,128)} %all-gather.2.cloned.1.call-done, f32[2,8,64,128]{3,2,1,0:T(8,128)S(1)} %bitcast.82), kind=kOutput, calls=%fused_computation.112 | convolution fusion | flops 100663296 | bytes 2625536 | tf_op jit(solution)/shard_map/dot_general | solution.py:62
  169.1 1.7 convolution_bitcast_fusion.6
  170.8 33.1 %psum.47 = f32[2,16,64]{2,1,0:T(8,128)S(1)} all-reduce(f32[2,16,64]{2,1,0:T(8,128)S(1)} %pad_maximum_fusion.8), channel_id=1, replica_groups=mesh['band'=4,'grid'=8] {'grid'}, use_global_device_ids=true, to_apply=%region_6.7 | all-reduce | flops 2048 | bytes 16384 | tf_op jit(solution)/shard_map/psum | solution.py:107
  (57 shorter events, 15.8 us)
Async XLA Ops:
  7.2 24.6 %copy-start.1 = (f32[16,8,8,128]{3,2,1,0:T(8,128)S(1)}, f32[16,8,8,128]{3,2,1,0:T(8,128)}, u32[]{:S(2)}) copy-start(f32[16,8,8,128]{3,2,1,0:T(8,128)} %param.5) | copy-start | bytes 1572868
  7.2 48.7 %copy-start.3 = (f32[8,8,128]{2,1,0:T(8,128)S(1)}, f32[8,8,128]{2,1,0:T(8,128)}, u32[]{:S(2)}) copy-start(f32[8,8,128]{2,1,0:T(8,128)} %param.6) | copy-start | bytes 98308
  7.2 48.7 %copy-start.4 = (f32[16]{0:T(128)S(1)}, f32[16]{0:T(128)}, u32[]{:S(2)}) copy-start(f32[16]{0:T(128)} %param.9) | copy-start | bytes 196
  7.2 158.4 %all-gather.2.cloned.1.call-start = ((), (), s32[]{:S(2)}) async-start(), calls=%async_computation | async-start | bytes 2621440 | tf_op jit(solution)/shard_map/all_gather | solution.py:105
  8.4 48.3 %collective-permute-start.1 = (f32[16,4,8,128]{3,2,1,0:T(8,128)S(1)}, f32[16,4,8,128]{3,2,1,0:T(8,128)S(1)}, u32[]{:S(2)}, u32[]{:S(2)}) collective-permute-start(f32[16,4,8,128]{3,2,1,0:T(8,128)S(1)} %get-tuple-element.14), channel_id=1, source_target_pairs={{0,1},{1,2},{2,3},{3,4},{4,5},{5,6},{6,7},{8,9},{9,10},{10,11},{11... | collective-permute-start | bytes 786440 | tf_op jit(solution)/shard_map/ppermute | solution.py:18
  13.3 43.6 %collective-permute-start = (f32[16,4,8,128]{3,2,1,0:T(8,128)S(1)}, f32[16,4,8,128]{3,2,1,0:T(8,128)S(1)}, u32[]{:S(2)}, u32[]{:S(2)}) collective-permute-start(f32[16,4,8,128]{3,2,1,0:T(8,128)S(1)} %get-tuple-element.13), channel_id=1, source_target_pairs={{1,0},{2,1},{3,2},{4,3},{5,4},{6,5},{7,6},{9,8},{10,9},{11,10},{12... | collective-permute-start | bytes 786440 | tf_op jit(solution)/shard_map/ppermute | solution.py:21
  58.8 24.8 %collective-permute-start.3 = (f32[16,4,8,128]{3,2,1,0:T(8,128)}, f32[16,4,8,128]{3,2,1,0:T(8,128)S(1)}, u32[]{:S(2)}, u32[]{:S(2)}) collective-permute-start(f32[16,4,8,128]{3,2,1,0:T(8,128)} %get-tuple-element.12), channel_id=1, source_target_pairs={{0,1},{1,2},{2,3},{3,4},{4,5},{5,6},{6,7},{8,9},{9,10},{10,11},{11... | collective-permute-start | bytes 786440 | tf_op jit(solution)/shard_map/ppermute | solution.py:18
  60.1 23.5 %collective-permute-start.2 = (f32[16,4,8,128]{3,2,1,0:T(8,128)S(1)}, f32[16,4,8,128]{3,2,1,0:T(8,128)S(1)}, u32[]{:S(2)}, u32[]{:S(2)}) collective-permute-start(f32[16,4,8,128]{3,2,1,0:T(8,128)S(1)} %get-tuple-element.11), channel_id=1, source_target_pairs={{1,0},{2,1},{3,2},{4,3},{5,4},{6,5},{7,6},{9,8},{10,9},{11,10},{12... | collective-permute-start | bytes 786440 | tf_op jit(solution)/shard_map/ppermute | solution.py:21
  85.0 24.8 %collective-permute-start.5 = (f32[16,4,8,128]{3,2,1,0:T(8,128)S(1)}, f32[16,4,8,128]{3,2,1,0:T(8,128)S(1)}, u32[]{:S(2)}, u32[]{:S(2)}) collective-permute-start(f32[16,4,8,128]{3,2,1,0:T(8,128)S(1)} %get-tuple-element.10), channel_id=1, source_target_pairs={{0,1},{1,2},{2,3},{3,4},{4,5},{5,6},{6,7},{8,9},{9,10},{10,11},{11... | collective-permute-start | bytes 786440 | tf_op jit(solution)/shard_map/ppermute | solution.py:18
  86.3 23.5 %collective-permute-start.4 = (f32[16,4,8,128]{3,2,1,0:T(8,128)S(1)}, f32[16,4,8,128]{3,2,1,0:T(8,128)S(1)}, u32[]{:S(2)}, u32[]{:S(2)}) collective-permute-start(f32[16,4,8,128]{3,2,1,0:T(8,128)S(1)} %get-tuple-element.9), channel_id=1, source_target_pairs={{1,0},{2,1},{3,2},{4,3},{5,4},{6,5},{7,6},{9,8},{10,9},{11,10},{12... | collective-permute-start | bytes 786440 | tf_op jit(solution)/shard_map/ppermute | solution.py:21
  111.1 25.1 %collective-permute-start.7 = (f32[16,4,8,128]{3,2,1,0:T(8,128)S(1)}, f32[16,4,8,128]{3,2,1,0:T(8,128)S(1)}, u32[]{:S(2)}, u32[]{:S(2)}) collective-permute-start(f32[16,4,8,128]{3,2,1,0:T(8,128)S(1)} %get-tuple-element.8), channel_id=1, source_target_pairs={{0,1},{1,2},{2,3},{3,4},{4,5},{5,6},{6,7},{8,9},{9,10},{10,11},{11... | collective-permute-start | bytes 786440 | tf_op jit(solution)/shard_map/ppermute | solution.py:18
  112.8 23.3 %collective-permute-start.6 = (f32[16,4,8,128]{3,2,1,0:T(8,128)S(1)}, f32[16,4,8,128]{3,2,1,0:T(8,128)S(1)}, u32[]{:S(2)}, u32[]{:S(2)}) collective-permute-start(f32[16,4,8,128]{3,2,1,0:T(8,128)S(1)} %get-tuple-element.7), channel_id=1, source_target_pairs={{1,0},{2,1},{3,2},{4,3},{5,4},{6,5},{7,6},{9,8},{10,9},{11,10},{12... | collective-permute-start | bytes 786440 | tf_op jit(solution)/shard_map/ppermute | solution.py:21
  137.5 28.1 %copy-start = (f32[16,8,8,128]{3,2,1,0:T(8,128)}, f32[16,8,8,128]{3,2,1,0:T(8,128)S(1)}, u32[]{:S(2)}) copy-start(f32[16,8,8,128]{3,2,1,0:T(8,128)S(1)} %fusion.45) | copy-start | bytes 1572868
  138.7 25.6 %collective-permute-start.9 = (f32[16,4,8,128]{3,2,1,0:T(8,128)S(1)}, f32[16,4,8,128]{3,2,1,0:T(8,128)S(1)}, u32[]{:S(2)}, u32[]{:S(2)}) collective-permute-start(f32[16,4,8,128]{3,2,1,0:T(8,128)S(1)} %get-tuple-element.6), channel_id=1, source_target_pairs={{0,1},{1,2},{2,3},{3,4},{4,5},{5,6},{6,7},{8,9},{9,10},{10,11},{11... | collective-permute-start | bytes 786440 | tf_op jit(solution)/shard_map/ppermute | solution.py:18
  140.2 24.1 %collective-permute-start.8 = (f32[16,4,8,128]{3,2,1,0:T(8,128)S(1)}, f32[16,4,8,128]{3,2,1,0:T(8,128)S(1)}, u32[]{:S(2)}, u32[]{:S(2)}) collective-permute-start(f32[16,4,8,128]{3,2,1,0:T(8,128)S(1)} %get-tuple-element.5), channel_id=1, source_target_pairs={{1,0},{2,1},{3,2},{4,3},{5,4},{6,5},{7,6},{9,8},{10,9},{11,10},{12... | collective-permute-start | bytes 786440 | tf_op jit(solution)/shard_map/ppermute | solution.py:21
  165.6 3.5 %copy-start.2 = (f32[64,8192]{1,0:T(8,128)S(1)}, f32[64,8192]{1,0:T(8,128)}, u32[]{:S(2)}) copy-start(f32[64,8192]{1,0:T(8,128)} %all-gather.2.cloned.1.call-done) | copy-start | bytes 6291460
Sparse Core Ops, SparseCore 0:
  138.7 20.3 all-gather.1
where the time goes:
time: 212 us; the launch traced here: 211 us
  blocking collectives  138 us (65%)
  other arithmetic  23.9 us (11%)
  starting transfers between devices  17.2 us (8%)
  between operations  14.5 us (7%)
  matrix products  13.6 us (6%)
  local copies, waits for them, and re-layouts  3.87 us (2%)
    psum x5, blocking collectives, apply_h(): coeffs = lax.psum(partial_value, 'grid')  105 us
    psum x1, blocking collectives, per_device(): blocks = lax.psum(partial_blocks, 'grid')  33.1 us
    unnamed x4, other arithmetic  15.6 us
    ppermute x5, starting transfers between devices, padded_2(): lax.ppermute(lax.slice_in_dim(block, block.shape[dim] - width, None, axis...  10.7 us
    dot_general x7, matrix products, inner_rows(): lax.dot_general(left, right, (((1,), (1,)), ((), ())), precision=lax.Prec...  10.1 us
    ppermute x5, starting transfers between devices, padded_2(): lax.ppermute(lax.slice_in_dim(block, 0, width, axis=dim), axis, backward)  6.46 us
  transfers between devices with their start and end apart: 11, of which 0 were waited for; matrix products, arithmetic and copies ran while one was open for 13% of the time, Pallas kernels for 0%

commit v1 on v0

--- a/solution.py
+++ b/solution.py
@@ -85,7 +85,7 @@
         kinetic_v = kinetic(padded)
         flat_v = field.reshape(state_count, points)
         partial_value = inner_rows(flat_v, projector)
-        coeffs = lax.psum(partial_value, "grid")
+        coeffs = jnp.sum(lax.all_gather(partial_value, "grid"), axis=0)
         scaled = coeffs * proj_strength[None, :]
         nonlocal_v = jnp.dot(
             scaled, projector, precision=lax.Precision.HIGHEST, preferred_element_type=jnp.float32

time: 212 us -> 278 us (1.31)
  blocking collectives: 138 us -> 195 us
  starting transfers between devices: 17.2 us -> 26.7 us
    all_gather x0 -> x5, blocking collectives: none -> 157 us  [apply_h(): coeffs = jnp.sum(lax.all_gather(partial_value, 'grid'), axis=0)]
    psum x5 -> x0, blocking collectives: 105 us -> none  [apply_h(): coeffs = lax.psum(partial_value, 'grid')]
    ppermute x5, starting transfers between devices: 10.7 us -> 20.2 us  [padded_2(): lax.ppermute(lax.slice_in_dim(block, block.shape[dim] - width, None, axis...]
    psum x1, blocking collectives: 33.1 us -> 37.6 us  [per_device(): blocks = lax.psum(partial_blocks, 'grid')]
  transfers between devices with their start and end apart: 11 -> 11, of which waited for: 0 -> 0; matrix products, arithmetic and copies ran while one was open for 13% -> 10% of each run, Pallas kernels for 0% -> 0%
where the time goes in v1:
time: 278 us
  blocking collectives  195 us (70%)
  starting transfers between devices  26.7 us (10%)
  other arithmetic  24 us (9%)
  between operations  14.5 us (5%)
  matrix products  13.5 us (5%)
  local copies, waits for them, and re-layouts  4.31 us (2%)
    all_gather x5, blocking collectives, apply_h(): coeffs = jnp.sum(lax.all_gather(partial_value, 'grid'), axis=0)  157 us
    psum x1, blocking collectives, per_device(): blocks = lax.psum(partial_blocks, 'grid')  37.6 us
    ppermute x5, starting transfers between devices, padded_2(): lax.ppermute(lax.slice_in_dim(block, block.shape[dim] - width, None, axis...  20.2 us
    unnamed x4, other arithmetic  15.6 us
    dot_general x7, matrix products, inner_rows(): lax.dot_general(left, right, (((1,), (1,)), ((), ())), precision=lax.Prec...  10 us
    ppermute x5, starting transfers between devices, padded_2(): lax.ppermute(lax.slice_in_dim(block, 0, width, axis=dim), axis, backward)  6.46 us
  transfers between devices with their start and end apart: 11, of which 0 were waited for; matrix products, arithmetic and copies ran while one was open for 10% of the time, Pallas kernels for 0%

profile of v1, /device:TPU:0, one launch (start us, length us, event | category | flops | bytes accessed | tf_op | source)
XLA Modules:
  0.0 277.7 jit_solution(1272269853869877625)
XLA Ops:
  8.4 4.9 %collective-permute-start.1 = (f32[16,4,8,128]{3,2,1,0:T(8,128)S(1)}, f32[16,4,8,128]{3,2,1,0:T(8,128)S(1)}, u32[]{:S(2)}, u32[]{:S(2)}) collective-permute-start(f32[16,4,8,128]{3,2,1,0:T(8,128)S(1)} %get-tuple-element.14), channel_id=1, source_target_pairs={{0,1},{1,2},{2,3},{3,4},{4,5},{5,6},{6,7},{8,9},{9,10},{10,11},{11... | collective-permute-start | bytes 786440 | tf_op jit(solution)/shard_map/ppermute | solution.py:18
  13.3 1.3 collective-permute-start
  17.5 14.1 %scatter_custom_fusion = f32[131072]{0:T(1024)S(1)} fusion(s32[2048]{0:T(1024)S(1)} %select_bitcast_fusion, f32[2048]{0:T(1024)S(1)} %select_bitcast_fusion.1, f32[]{:T(128)} %constant.17.clone.1), kind=kCustom, calls=%fused_computation.348 | custom fusion | flops 2048 | bytes 524292
  32.8 32.1 %all-gather = f32[128,16]{1,0:T(8,128)S(1)} all-gather(f32[16,16]{1,0:T(8,128)S(1)} %copy.10), channel_id=2, replica_groups=mesh['band'=4,'grid'=8] {'grid'}, dimensions={0}, use_global_device_ids=true | all-gather | bytes 9216 | tf_op jit(solution)/shard_map/all_gather | solution.py:88
  66.0 1.2 broadcast_multiply_fusion
  67.9 3.4 %collective-permute-start.3 = (f32[16,4,8,128]{3,2,1,0:T(8,128)}, f32[16,4,8,128]{3,2,1,0:T(8,128)S(1)}, u32[]{:S(2)}, u32[]{:S(2)}) collective-permute-start(f32[16,4,8,128]{3,2,1,0:T(8,128)} %get-tuple-element.12), channel_id=1, source_target_pairs={{0,1},{1,2},{2,3},{3,4},{4,5},{5,6},{6,7},{8,9},{9,10},{10,11},{11... | collective-permute-start | bytes 786440 | tf_op jit(solution)/shard_map/ppermute | solution.py:18
  71.3 1.3 collective-permute-start.2
  73.6 31.3 %all-gather.1 = f32[128,16]{1,0:T(8,128)S(1)} all-gather(f32[16,16]{1,0:T(8,128)S(1)} %fusion.189), channel_id=3, replica_groups=mesh['band'=4,'grid'=8] {'grid'}, dimensions={0}, use_global_device_ids=true | all-gather | bytes 9216 | tf_op jit(solution)/shard_map/all_gather | solution.py:88
  105.8 1.3 fusion.113
  107.1 3.9 %collective-permute-start.5 = (f32[16,4,8,128]{3,2,1,0:T(8,128)S(1)}, f32[16,4,8,128]{3,2,1,0:T(8,128)S(1)}, u32[]{:S(2)}, u32[]{:S(2)}) collective-permute-start(f32[16,4,8,128]{3,2,1,0:T(8,128)S(1)} %get-tuple-element.10), channel_id=1, source_target_pairs={{0,1},{1,2},{2,3},{3,4},{4,5},{5,6},{6,7},{8,9},{9,10},{10,11},{11... | collective-permute-start | bytes 786440 | tf_op jit(solution)/shard_map/ppermute | solution.py:18
  111.1 1.3 collective-permute-start.4
  113.3 31.2 %all-gather.2 = f32[128,16]{1,0:T(8,128)S(1)} all-gather(f32[16,16]{1,0:T(8,128)S(1)} %fusion.186), channel_id=4, replica_groups=mesh['band'=4,'grid'=8] {'grid'}, dimensions={0}, use_global_device_ids=true | all-gather | bytes 9216 | tf_op jit(solution)/shard_map/all_gather | solution.py:88
  145.5 1.3 fusion.79
  146.8 4.0 %collective-permute-start.7 = (f32[16,4,8,128]{3,2,1,0:T(8,128)S(1)}, f32[16,4,8,128]{3,2,1,0:T(8,128)S(1)}, u32[]{:S(2)}, u32[]{:S(2)}) collective-permute-start(f32[16,4,8,128]{3,2,1,0:T(8,128)S(1)} %get-tuple-element.8), channel_id=1, source_target_pairs={{0,1},{1,2},{2,3},{3,4},{4,5},{5,6},{6,7},{8,9},{9,10},{10,11},{11... | collective-permute-start | bytes 786440 | tf_op jit(solution)/shard_map/ppermute | solution.py:18
  150.8 1.3 collective-permute-start.6
  153.0 31.3 %all-gather.3 = f32[128,16]{1,0:T(8,128)S(1)} all-gather(f32[16,16]{1,0:T(8,128)S(1)} %fusion.183), channel_id=5, replica_groups=mesh['band'=4,'grid'=8] {'grid'}, dimensions={0}, use_global_device_ids=true | all-gather | bytes 9216 | tf_op jit(solution)/shard_map/all_gather | solution.py:88
  185.3 1.3 fusion.45
  187.8 3.9 %collective-permute-start.9 = (f32[16,4,8,128]{3,2,1,0:T(8,128)S(1)}, f32[16,4,8,128]{3,2,1,0:T(8,128)S(1)}, u32[]{:S(2)}, u32[]{:S(2)}) collective-permute-start(f32[16,4,8,128]{3,2,1,0:T(8,128)S(1)} %get-tuple-element.6), channel_id=1, source_target_pairs={{0,1},{1,2},{2,3},{3,4},{4,5},{5,6},{6,7},{8,9},{9,10},{10,11},{11... | collective-permute-start | bytes 786440 | tf_op jit(solution)/shard_map/ppermute | solution.py:18
  191.7 1.3 collective-permute-start.8
  194.0 31.1 %all-gather.4 = f32[128,16]{1,0:T(8,128)S(1)} all-gather(f32[16,16]{1,0:T(8,128)S(1)} %fusion.213), channel_id=6, replica_groups=mesh['band'=4,'grid'=8] {'grid'}, dimensions={0}, use_global_device_ids=true | all-gather | bytes 9216 | tf_op jit(solution)/shard_map/all_gather | solution.py:88
  226.1 1.3 fusion.11
  227.4 3.5 %convolution_bitcast_fusion.7 = f32[1,16,64]{2,1,0:T(8,128)S(1)} fusion(f32[64,8192]{1,0:T(8,128)} %all-gather.7.cloned.1.call-done, f32[2,8,64,128]{3,2,1,0:T(8,128)S(1)} %bitcast.87), kind=kOutput, calls=%fused_computation.112 | convolution fusion | flops 100663296 | bytes 2625536 | tf_op jit(solution)/shard_map/dot_general | solution.py:62
  230.9 1.7 convolution_bitcast_fusion.6
  232.7 37.6 %psum.7 = f32[2,16,64]{2,1,0:T(8,128)S(1)} all-reduce(f32[2,16,64]{2,1,0:T(8,128)S(1)} %pad_maximum_fusion.8), channel_id=1, replica_groups=mesh['band'=4,'grid'=8] {'grid'}, use_global_device_ids=true, to_apply=%region_6.7 | all-reduce | flops 2048 | bytes 16384 | tf_op jit(solution)/shard_map/psum | solution.py:107
  (68 shorter events, 16.3 us)
Async XLA Ops:
  7.2 24.6 %copy-start.1 = (f32[16,8,8,128]{3,2,1,0:T(8,128)S(1)}, f32[16,8,8,128]{3,2,1,0:T(8,128)}, u32[]{:S(2)}) copy-start(f32[16,8,8,128]{3,2,1,0:T(8,128)} %param.5) | copy-start | bytes 1572868
  7.2 57.8 %copy-start.3 = (f32[8,8,128]{2,1,0:T(8,128)S(1)}, f32[8,8,128]{2,1,0:T(8,128)}, u32[]{:S(2)}) copy-start(f32[8,8,128]{2,1,0:T(8,128)} %param.6) | copy-start | bytes 98308
  7.2 57.8 %copy-start.4 = (f32[16]{0:T(128)S(1)}, f32[16]{0:T(128)}, u32[]{:S(2)}) copy-start(f32[16]{0:T(128)} %param.9) | copy-start | bytes 196
  7.2 220.2 %all-gather.7.cloned.1.call-start = ((), (), s32[]{:S(2)}) async-start(), calls=%async_computation | async-start | bytes 2621440 | tf_op jit(solution)/shard_map/all_gather | solution.py:105
  8.4 57.4 %collective-permute-start.1 = (f32[16,4,8,128]{3,2,1,0:T(8,128)S(1)}, f32[16,4,8,128]{3,2,1,0:T(8,128)S(1)}, u32[]{:S(2)}, u32[]{:S(2)}) collective-permute-start(f32[16,4,8,128]{3,2,1,0:T(8,128)S(1)} %get-tuple-element.14), channel_id=1, source_target_pairs={{0,1},{1,2},{2,3},{3,4},{4,5},{5,6},{6,7},{8,9},{9,10},{10,11},{11... | collective-permute-start | bytes 786440 | tf_op jit(solution)/shard_map/ppermute | solution.py:18
  13.3 52.7 %collective-permute-start = (f32[16,4,8,128]{3,2,1,0:T(8,128)S(1)}, f32[16,4,8,128]{3,2,1,0:T(8,128)S(1)}, u32[]{:S(2)}, u32[]{:S(2)}) collective-permute-start(f32[16,4,8,128]{3,2,1,0:T(8,128)S(1)} %get-tuple-element.13), channel_id=1, source_target_pairs={{1,0},{2,1},{3,2},{4,3},{5,4},{6,5},{7,6},{9,8},{10,9},{11,10},{12... | collective-permute-start | bytes 786440 | tf_op jit(solution)/shard_map/ppermute | solution.py:21
  67.9 37.9 %collective-permute-start.3 = (f32[16,4,8,128]{3,2,1,0:T(8,128)}, f32[16,4,8,128]{3,2,1,0:T(8,128)S(1)}, u32[]{:S(2)}, u32[]{:S(2)}) collective-permute-start(f32[16,4,8,128]{3,2,1,0:T(8,128)} %get-tuple-element.12), channel_id=1, source_target_pairs={{0,1},{1,2},{2,3},{3,4},{4,5},{5,6},{6,7},{8,9},{9,10},{10,11},{11... | collective-permute-start | bytes 786440 | tf_op jit(solution)/shard_map/ppermute | solution.py:18
  71.3 34.4 %collective-permute-start.2 = (f32[16,4,8,128]{3,2,1,0:T(8,128)S(1)}, f32[16,4,8,128]{3,2,1,0:T(8,128)S(1)}, u32[]{:S(2)}, u32[]{:S(2)}) collective-permute-start(f32[16,4,8,128]{3,2,1,0:T(8,128)S(1)} %get-tuple-element.11), channel_id=1, source_target_pairs={{1,0},{2,1},{3,2},{4,3},{5,4},{6,5},{7,6},{9,8},{10,9},{11,10},{12... | collective-permute-start | bytes 786440 | tf_op jit(solution)/shard_map/ppermute | solution.py:21
  107.1 38.3 %collective-permute-start.5 = (f32[16,4,8,128]{3,2,1,0:T(8,128)S(1)}, f32[16,4,8,128]{3,2,1,0:T(8,128)S(1)}, u32[]{:S(2)}, u32[]{:S(2)}) collective-permute-start(f32[16,4,8,128]{3,2,1,0:T(8,128)S(1)} %get-tuple-element.10), channel_id=1, source_target_pairs={{0,1},{1,2},{2,3},{3,4},{4,5},{5,6},{6,7},{8,9},{9,10},{10,11},{11... | collective-permute-start | bytes 786440 | tf_op jit(solution)/shard_map/ppermute | solution.py:18
  111.1 34.4 %collective-permute-start.4 = (f32[16,4,8,128]{3,2,1,0:T(8,128)S(1)}, f32[16,4,8,128]{3,2,1,0:T(8,128)S(1)}, u32[]{:S(2)}, u32[]{:S(2)}) collective-permute-start(f32[16,4,8,128]{3,2,1,0:T(8,128)S(1)} %get-tuple-element.9), channel_id=1, source_target_pairs={{1,0},{2,1},{3,2},{4,3},{5,4},{6,5},{7,6},{9,8},{10,9},{11,10},{12... | collective-permute-start | bytes 786440 | tf_op jit(solution)/shard_map/ppermute | solution.py:21
  146.8 38.5 %collective-permute-start.7 = (f32[16,4,8,128]{3,2,1,0:T(8,128)S(1)}, f32[16,4,8,128]{3,2,1,0:T(8,128)S(1)}, u32[]{:S(2)}, u32[]{:S(2)}) collective-permute-start(f32[16,4,8,128]{3,2,1,0:T(8,128)S(1)} %get-tuple-element.8), channel_id=1, source_target_pairs={{0,1},{1,2},{2,3},{3,4},{4,5},{5,6},{6,7},{8,9},{9,10},{10,11},{11... | collective-permute-start | bytes 786440 | tf_op jit(solution)/shard_map/ppermute | solution.py:18
  150.8 34.5 %collective-permute-start.6 = (f32[16,4,8,128]{3,2,1,0:T(8,128)S(1)}, f32[16,4,8,128]{3,2,1,0:T(8,128)S(1)}, u32[]{:S(2)}, u32[]{:S(2)}) collective-permute-start(f32[16,4,8,128]{3,2,1,0:T(8,128)S(1)} %get-tuple-element.7), channel_id=1, source_target_pairs={{1,0},{2,1},{3,2},{4,3},{5,4},{6,5},{7,6},{9,8},{10,9},{11,10},{12... | collective-permute-start | bytes 786440 | tf_op jit(solution)/shard_map/ppermute | solution.py:21
  186.6 40.8 %copy-start = (f32[16,8,8,128]{3,2,1,0:T(8,128)}, f32[16,8,8,128]{3,2,1,0:T(8,128)S(1)}, u32[]{:S(2)}) copy-start(f32[16,8,8,128]{3,2,1,0:T(8,128)S(1)} %fusion.45) | copy-start | bytes 1572868
  187.8 38.3 %collective-permute-start.9 = (f32[16,4,8,128]{3,2,1,0:T(8,128)S(1)}, f32[16,4,8,128]{3,2,1,0:T(8,128)S(1)}, u32[]{:S(2)}, u32[]{:S(2)}) collective-permute-start(f32[16,4,8,128]{3,2,1,0:T(8,128)S(1)} %get-tuple-element.6), channel_id=1, source_target_pairs={{0,1},{1,2},{2,3},{3,4},{4,5},{5,6},{6,7},{8,9},{9,10},{10,11},{11... | collective-permute-start | bytes 786440 | tf_op jit(solution)/shard_map/ppermute | solution.py:18
  191.7 34.3 %collective-permute-start.8 = (f32[16,4,8,128]{3,2,1,0:T(8,128)S(1)}, f32[16,4,8,128]{3,2,1,0:T(8,128)S(1)}, u32[]{:S(2)}, u32[]{:S(2)}) collective-permute-start(f32[16,4,8,128]{3,2,1,0:T(8,128)S(1)} %get-tuple-element.5), channel_id=1, source_target_pairs={{1,0},{2,1},{3,2},{4,3},{5,4},{6,5},{7,6},{9,8},{10,9},{11,10},{12... | collective-permute-start | bytes 786440 | tf_op jit(solution)/shard_map/ppermute | solution.py:21
  227.4 3.5 %copy-start.2 = (f32[64,8192]{1,0:T(8,128)S(1)}, f32[64,8192]{1,0:T(8,128)}, u32[]{:S(2)}) copy-start(f32[64,8192]{1,0:T(8,128)} %all-gather.7.cloned.1.call-done) | copy-start | bytes 6291460
Sparse Core Ops, SparseCore 0:
  187.9 23.9 all-gather.6
